TPU v7x, 32 devices: a whole 2x2x4 slice. The times are simulated.
32 devices in a mesh: grp: 2 (over y), leaf: 16 (over z, x, core).
Axes of the slice: x: 2, y: 2, z: 4, core: 2. Of those that a mesh axis runs over, the one named last changes fastest.
Arguments:
- vectors: float32 [16, 32768], P(None, ('grp', 'leaf')), may hold values from -6 to 6
- points: float32 [3, 32768], P(None, ('grp', 'leaf')), may hold values from -1 to 2
- near_lists: int32 [64, 6], P(('grp', 'leaf')), may hold values from -1 to 5, as said below
- inter_lists: int32 [64, 16], P(('grp', 'leaf')), may hold values from 0 to 31, as said below
- skeleton: int32 [64, 64], P(('grp', 'leaf')), may hold values from 0 to 511, as said below
- interp: float32 [64, 64, 512], P(('grp', 'leaf')), may hold values from -0.25 to 0.25
- transfer: float32 [64, 64, 128], P(('grp', 'leaf')), may hold values from -0.125 to 0.125
- coarse_points: float32 [2, 3, 128], replicated, may hold values from 0 to 1
Outputs:
- filtered: float32 [16, 32768], P(None, ('grp', 'leaf'))
Inputs may be any that keep to these rules, and one draw needn't show every extreme that they name: `near_lists`: place w of leaf l's window is leaf (l // 2 - 1) * 2 + w. Slot 0 holds the leaf itself (2 + l % 2); the next slots hold distinct places of other leaves of the same subtree; then -1 to the end of the row. `inter_lists`: distinct leaves of the leaf's own subtree, numbered from the subtree's first leaf, none in the leaf's window. `skeleton`: distinct places within the leaf.
All inputs are finite; a program needn't handle non-finite values.
Results may differ from a plain program's by a relative error of at most 0.00013.
Values sent between devices are 32-bit elements; how exact they have to be, the bound alone decides.
No kernel may reach another device: no remote copies, remote signals or barrier semaphores. Data moves between devices by JAX's collectives and lax.ppermute only.
A program may use at most 64 MiB of HBM per device.

v0:
```python
import jax
import jax.numpy as jnp
from jax import lax
from jax.sharding import PartitionSpec as P

kappa_scale = 3.4641016151377544
centre = 0.05
half_width = 0.05
highest = lax.Precision.HIGHEST


def with_halo(x, sides, width):
    for axis, dim in sides:
        devices, length = (lax.axis_size(axis), x.shape[dim])
        up = [(i, (i + 1) % devices) for i in range(devices - 1)]
        down = [(j, i) for i, j in up]
        last = lax.slice_in_dim(x, length - width, length, axis=dim)
        initial = lax.slice_in_dim(x, 0, width, axis=dim)
        before = lax.ppermute(last, axis, up)
        after = lax.ppermute(initial, axis, down)
        x = jnp.concatenate([before, x, after], axis=dim)
    return x


def matern(source, target):
    delta_x = source[..., 0, :, None] - target[..., 0, None, :]
    delta_y = source[..., 1, :, None] - target[..., 1, None, :]
    delta_z = source[..., 2, :, None] - target[..., 2, None, :]
    scaled = kappa_scale * jnp.sqrt(delta_x * delta_x + delta_y * delta_y + delta_z * delta_z)
    return (1.0 + scaled) * jnp.exp(-scaled)


def on_device(vectors, points, near_lists, inter_lists, skeleton, interp, transfer, coarse_points):
    per_dev = near_lists.shape[0]
    slot_count = near_lists.shape[1]
    leaf_size = interp.shape[2]
    vec_count = vectors.shape[0]
    leaf_index = lax.axis_index("leaf")
    group_index = lax.axis_index("grp")
    group_count = lax.axis_size("grp")
    leaf_points = points.reshape(3, per_dev, leaf_size).transpose(1, 0, 2)
    skel_points = jnp.take_along_axis(leaf_points, skeleton[:, None, :], axis=2)
    subtree_skel = lax.all_gather(skel_points, "leaf", axis=0, tiled=True)
    own_coarse = lax.dynamic_index_in_dim(coarse_points, group_index, 0, keepdims=False)
    apart = (jnp.arange(group_count) != group_index).astype(jnp.float32)
    coupling = matern(coarse_points, own_coarse[None]) * apart[:, None, None]
    live_slots = jnp.max(jnp.sum((near_lists >= 0).astype(jnp.int32), axis=1))
    first_leaf = leaf_index * per_dev
    subtree_lists = lax.all_gather(inter_lists, "leaf", axis=0, tiled=True)
    own_ids = first_leaf + jnp.arange(per_dev, dtype=jnp.int32)
    hits = jnp.sum(
        (subtree_lists[:, :, None] == own_ids[None, None, :]).astype(jnp.float32), axis=1
    )
    push_kernel = matern(skel_points[None], subtree_skel[:, None]) * hits[:, :, None, None]

    def operate(field):
        stacked = jnp.concatenate([points, field], axis=0)
        window = with_halo(stacked, (("leaf", 1),), per_dev * leaf_size)
        window_points = window[:3].reshape(3, 3 * per_dev, leaf_size)
        window_vecs = window[3:].reshape(vec_count, 3 * per_dev, leaf_size)

        def near_slot(slot, running):
            chosen = lax.dynamic_index_in_dim(near_lists, slot, 1, keepdims=False)
            present = (chosen >= 0).astype(jnp.float32)
            safe_place = jnp.where(chosen >= 0, chosen, 0)
            source_points = jnp.take(window_points, safe_place, axis=1).transpose(1, 0, 2)
            source_vecs = jnp.take(window_vecs, safe_place, axis=1)
            kernel = matern(source_points, leaf_points)
            product = jnp.einsum("vlp,lpq->lvq", source_vecs, kernel, precision=highest)
            return running + present[:, None, None] * product

        near_part = lax.fori_loop(
            0, live_slots, near_slot, jnp.zeros((per_dev, vec_count, leaf_size), jnp.float32)
        )
        leaf_vecs = field.reshape(vec_count, per_dev, leaf_size)
        coeffs = jnp.einsum("vlp,lrp->lvr", leaf_vecs, interp, precision=highest)
        leaf_far = lax.psum_scatter(
            jnp.einsum("jvr,tjrq->tvq", coeffs, push_kernel, precision=highest),
            "leaf",
            scatter_dimension=0,
            tiled=True,
        )
        upward = jnp.einsum("lvr,lrc->vc", coeffs, transfer, precision=highest)
        subtree_total = lax.psum(upward, "leaf")
        group_coeffs = lax.all_gather(subtree_total[None], "grp", axis=0, tiled=True)
        coarse_field = jnp.einsum("avr,arq->vq", group_coeffs, coupling, precision=highest)
        downward = leaf_far + jnp.einsum("vc,lrc->lvr", coarse_field, transfer, precision=highest)
        far_part = jnp.einsum("lvr,lrp->lvp", downward, interp, precision=highest)
        combined = (near_part + far_part) / (leaf_size * slot_count)
        return combined.transpose(1, 0, 2).reshape(vec_count, per_dev * leaf_size)

    term_one = (operate(vectors) - centre * vectors) / half_width
    term_two = 2.0 * (operate(term_one) - centre * term_one) / half_width - vectors
    term_three = 2.0 * (operate(term_two) - centre * term_two) / half_width - term_one
    squares = lax.psum(jnp.sum(term_three * term_three, axis=1), ("grp", "leaf"))
    total_points = vectors.shape[1] * group_count * lax.axis_size("leaf")
    return term_three / jnp.sqrt(squares / total_points + 1e-06)[:, None]


def solution(mesh):
    placed = (
        P(None, ("grp", "leaf")),
        P(None, ("grp", "leaf")),
        P(("grp", "leaf"), None),
        P(("grp", "leaf"), None),
        P(("grp", "leaf"), None),
        P(("grp", "leaf"), None, None),
        P(("grp", "leaf"), None, None),
        P(),
    )
    return jax.shard_map(
        on_device, mesh=mesh, in_specs=placed, out_specs=P(None, ("grp", "leaf")), check_vma=False
    )
```

profile of v0, /device:TPU:10, one launch (start us, length us, event | category | flops | bytes accessed | tf_op | source)
XLA Modules:
  0.0 312.5 jit_solution(3287674258489741425)
XLA Ops:
  6.5 0.9 pad_maximum_fusion.3
  7.5 2.1 collective-permute-start.1
  9.5 2.4 collective-permute-start
  11.9 0.9 copy.61
  13.0 1.2 gather_fusion.6
  14.4 15.5 %all-gather = s32[16,2,16]{2,1,0:T(2,128)S(1)} all-gather(s32[1,2,16]{2,1,0:T(2,128)S(1)} %bitcast.260), channel_id=1, replica_groups=mesh['grp'=2,'leaf'=16] {'leaf'}, dimensions={0}, use_global_device_ids=true | all-gather | bytes 2176 | tf_op jit(solution)/shard_map/all_gather | solution.py:49
  30.1 21.1 %all_gather.15 = f32[32,3,64]{2,1,0:T(4,128)S(1)} all-gather(f32[2,3,64]{2,1,0:T(4,128)S(1)} %bitcast_select_fusion.1), channel_id=1, replica_groups=mesh['grp'=2,'leaf'=16] {'leaf'}, dimensions={0}, use_global_device_ids=true | all-gather | bytes 26112 | tf_op jit(solution)/shard_map/all_gather | solution.py:43
  51.6 3.5 %convolution_bitcast_fusion.2 = f32[32,16,64]{2,1,0:T(8,128)} fusion(f32[32,2]{1,0:T(8,128)S(1)} %copy.67, f32[32,64]{1,0:T(8,128)S(1)} %bitcast.254, f32[2,64]{1,0:T(2,128)S(1)} %bitcast.264, f32[32,64]{1,0:T(8,128)S(1)} %bitcast.257, f32[2,64]{1,0:T(2,128)S(1)} %bitcast.267, f32[32,64]{1,0:T(8,128)S(1)} %bitcast.251, f32[2,64]{1,0:T(2,128)S(1)} %bitcast.261, ...), kind=kOutput, calls=%fused_computation.145 | convolution fusion | flops 53739520 | bytes 165632 | tf_op jit(solution)/shard_map/jvr,tjrq->tvq/dot_general | solution.py:78
  56.1 24.3 %psum.28 = f32[1,16,128]{2,1,0:T(8,128)S(1)} all-reduce(f32[1,16,128]{2,1,0:T(8,128)S(1)} %convolution_bitcast_fusion.8), channel_id=1, replica_groups=mesh['grp'=2,'leaf'=16] {'leaf'}, use_global_device_ids=true, to_apply=%region_6.9 | all-reduce | flops 2048 | bytes 16384 | tf_op jit(solution)/shard_map/psum | solution.py:84
  80.4 4.4 %all_gather.17 = f32[2,16,128]{2,1,0:T(8,128)S(1)} all-gather(f32[1,16,128]{2,1,0:T(8,128)S(1)} %psum.28), channel_id=1, replica_groups=mesh['grp'=2,'leaf'=16] {'grp'}, dimensions={0}, use_global_device_ids=true | all-gather | bytes 24576 | tf_op jit(solution)/shard_map/all_gather | solution.py:85
  85.3 0.6 reduce_max.9
  86.1 28.6 %while.30 = (s32[]{:T(128)}, f32[2,16,512]{2,1,0:T(8,128)S(1)}, s32[]{:T(128)}, s32[2,6]{0,1:T(8,128)S(1)}, f32[16,6,512]{2,0,1:T(8,128)S(1)}, /*index=5*/f32[3,...) while((s32[]{:T(128)}, f32[2,16,512]{2,1,0:T(8,128)S(1)}, s32[]{:T(128)}, ...), condition=%wide.region_3.0_spmd, body=%wide.region_2.0_spmd.sunk | while | flops 107008024 | bytes 479441 | solution.py:72
  86.7 0.6 gather_fusion
  87.9 2.8 fusion.199
  91.4 0.6 gather_fusion
  92.6 2.8 fusion.199
  96.0 0.6 gather_fusion
  97.3 2.8 fusion.199
  100.7 0.6 gather_fusion
  102.0 2.8 fusion.199
  105.4 0.6 gather_fusion
  106.6 2.8 fusion.199
  110.1 0.6 gather_fusion
  111.3 2.8 fusion.199
  114.7 0.9 fusion.116
  116.0 1.9 collective-permute-start.3
  117.9 2.4 collective-permute-start.2
  120.7 3.5 %convolution_bitcast_fusion.1 = f32[32,16,64]{2,1,0:T(8,128)} fusion(f32[32,2]{1,0:T(8,128)S(1)} %copy.67, f32[32,64]{1,0:T(8,128)S(1)} %bitcast.255, f32[2,64]{1,0:T(2,128)S(1)} %bitcast.265, f32[32,64]{1,0:T(8,128)S(1)} %bitcast.258, f32[2,64]{1,0:T(2,128)S(1)} %bitcast.268, f32[32,64]{1,0:T(8,128)S(1)} %bitcast.252, f32[2,64]{1,0:T(2,128)S(1)} %bitcast.262, ...), kind=kOutput, calls=%fused_computation.144 | convolution fusion | flops 53739520 | bytes 165632 | tf_op jit(solution)/shard_map/jvr,tjrq->tvq/dot_general | solution.py:78
  124.4 26.7 %psum.29 = f32[1,16,128]{2,1,0:T(8,128)S(1)} all-reduce(f32[1,16,128]{2,1,0:T(8,128)S(1)} %convolution_bitcast_fusion.7), channel_id=1, replica_groups=mesh['grp'=2,'leaf'=16] {'leaf'}, use_global_device_ids=true, to_apply=%region_10.13 | all-reduce | flops 2048 | bytes 16384 | tf_op jit(solution)/shard_map/psum | solution.py:84
  151.2 4.4 %all_gather.18 = f32[2,16,128]{2,1,0:T(8,128)S(1)} all-gather(f32[1,16,128]{2,1,0:T(8,128)S(1)} %psum.29), channel_id=1, replica_groups=mesh['grp'=2,'leaf'=16] {'grp'}, dimensions={0}, use_global_device_ids=true | all-gather | bytes 24576 | tf_op jit(solution)/shard_map/all_gather | solution.py:85
  156.0 28.8 %while.31 = (s32[]{:T(128)}, f32[2,16,512]{2,1,0:T(8,128)S(1)}, s32[]{:T(128)}, s32[2,6]{0,1:T(8,128)S(1)}, f32[16,6,512]{2,0,1:T(8,128)S(1)}, /*index=5*/f32[3,...) while((s32[]{:T(128)}, f32[2,16,512]{2,1,0:T(8,128)S(1)}, s32[]{:T(128)}, ...), condition=%wide.region_8.11_spmd, body=%wide.region_7.10_spmd.sunk | while | flops 107008024 | bytes 479441 | solution.py:72
  156.8 0.6 gather_fusion.2
  158.1 2.8 fusion.203
  161.5 0.6 gather_fusion.2
  162.7 2.8 fusion.203
  166.2 0.6 gather_fusion.2
  167.4 2.8 fusion.203
  170.8 0.6 gather_fusion.2
  172.1 2.8 fusion.203
  175.5 0.6 gather_fusion.2
  176.8 2.8 fusion.203
  180.2 0.6 gather_fusion.2
  181.4 2.8 fusion.203
  185.3 0.9 fusion.115
  186.6 1.9 collective-permute-start.5
  188.5 2.4 collective-permute-start.4
  191.3 3.5 %convolution_bitcast_fusion = f32[32,16,64]{2,1,0:T(8,128)} fusion(f32[32,2]{1,0:T(8,128)S(1)} %copy.67, f32[32,64]{1,0:T(8,128)S(1)} %bitcast.256, f32[2,64]{1,0:T(2,128)S(1)} %bitcast.266, f32[32,64]{1,0:T(8,128)S(1)} %bitcast.259, f32[2,64]{1,0:T(2,128)S(1)} %bitcast.269, f32[32,64]{1,0:T(8,128)S(1)} %bitcast.253, f32[2,64]{1,0:T(2,128)S(1)} %bitcast.263, ...), kind=kOutput, calls=%fused_computation.143 | convolution fusion | flops 53739520 | bytes 165632 | tf_op jit(solution)/shard_map/jvr,tjrq->tvq/dot_general | solution.py:78
  195.0 28.1 %psum.30 = f32[1,16,128]{2,1,0:T(8,128)S(1)} all-reduce(f32[1,16,128]{2,1,0:T(8,128)S(1)} %convolution_bitcast_fusion.6), channel_id=1, replica_groups=mesh['grp'=2,'leaf'=16] {'leaf'}, use_global_device_ids=true, to_apply=%region_14.17 | all-reduce | flops 2048 | bytes 16384 | tf_op jit(solution)/shard_map/psum | solution.py:84
  223.1 4.4 %all_gather.19 = f32[2,16,128]{2,1,0:T(8,128)S(1)} all-gather(f32[1,16,128]{2,1,0:T(8,128)S(1)} %psum.30), channel_id=1, replica_groups=mesh['grp'=2,'leaf'=16] {'grp'}, dimensions={0}, use_global_device_ids=true | all-gather | bytes 24576 | tf_op jit(solution)/shard_map/all_gather | solution.py:85
  227.9 28.6 %while.32 = (s32[]{:T(128)}, f32[2,16,512]{2,1,0:T(8,128)S(1)}, s32[]{:T(128)}, s32[2,6]{0,1:T(8,128)S(1)}, f32[16,6,512]{2,0,1:T(8,128)S(1)}, /*index=5*/f32[3,...) while((s32[]{:T(128)}, f32[2,16,512]{2,1,0:T(8,128)S(1)}, s32[]{:T(128)}, ...), condition=%wide.region_12.15_spmd, body=%wide.region_11.14_spmd.sunk | while | flops 107008024 | bytes 479441 | solution.py:72
  228.6 0.6 gather_fusion.4
  229.8 2.8 fusion.207
  233.2 0.6 gather_fusion.4
  234.5 2.8 fusion.207
  237.9 0.6 gather_fusion.4
  239.2 2.8 fusion.207
  242.6 0.6 gather_fusion.4
  243.8 2.8 fusion.207
  248.5 2.8 fusion.207
  253.2 2.8 fusion.207
  256.6 0.7 reduce-scatter.8.cloned.1.call-done
  257.3 0.9 fusion.114
  258.7 46.5 %psum.31 = f32[16]{0:T(128)S(1)} all-reduce(f32[16]{0:T(128)S(1)} %multiply_reduce_fusion), channel_id=1, replica_groups=mesh['grp'=2,'leaf'=16] {'grp','leaf'}, use_global_device_ids=true, to_apply=%region_16.19 | all-reduce | flops 16 | bytes 128 | tf_op jit(solution)/shard_map/psum | solution.py:95
  305.2 0.7 broadcast_divide_fusion
  (212 shorter events, 19.1 us)
Async XLA Ops:
  6.5 44.8 %copy-start = (f32[2,64,512]{2,1,0:T(8,128)S(1)}, f32[2,64,512]{2,1,0:T(8,128)}, u32[]{:S(2)}) copy-start(f32[2,64,512]{2,1,0:T(8,128)} %param.23) | copy-start | bytes 786436
  6.5 6.4 %copy-start.7 = (s32[2,64]{1,0:T(2,128)S(1)}, s32[2,64]{1,0:T(2,128)}, u32[]{:S(2)}) copy-start(s32[2,64]{1,0:T(2,128)} %param.22) | copy-start | bytes 1540
  6.5 7.8 %copy-start.5 = (s32[2,16]{1,0:T(2,128)S(1)}, s32[2,16]{1,0:T(2,128)}, u32[]{:S(2)}) copy-start(s32[2,16]{1,0:T(2,128)} %param.21) | copy-start | bytes 388
  6.5 108.2 %reduce-scatter.4.cloned.1.call-start = ((), (), s32[]{:S(2)}) async-start(), calls=%async_computation.3 | async-start | bytes 278528 | tf_op jit(solution)/shard_map/reduce_scatter | solution.py:77
  7.5 43.8 %copy-start.2 = (f32[16,1024]{1,0:T(8,128)S(1)}, f32[16,1024]{1,0:T(8,128)}, u32[]{:S(2)}) copy-start(f32[16,1024]{1,0:T(8,128)} %param.18) | copy-start | bytes 196612
  7.5 78.5 %collective-permute-start.1 = (f32[19,1024]{1,0:T(8,128)S(1)}, f32[19,1024]{1,0:T(8,128)S(1)}, u32[]{:S(2)}, u32[]{:S(2)}) collective-permute-start(f32[19,1024]{1,0:T(8,128)S(1)} %pad_maximum_fusion.3), channel_id=1, source_target_pairs={{1,0},{2,1},{3,2},{4,3},{5,4},{6,5},{7,6},{8,7},{9,8},{10,9},{11,1... | collective-permute-start | bytes 233480 | tf_op jit(solution)/shard_map/ppermute | solution.py:20
  9.5 76.4 %collective-permute-start = (f32[19,1024]{1,0:T(8,128)S(1)}, f32[19,1024]{1,0:T(8,128)S(1)}, u32[]{:S(2)}, u32[]{:S(2)}) collective-permute-start(f32[19,1024]{1,0:T(8,128)S(1)} %pad_maximum_fusion.3), channel_id=1, source_target_pairs={{0,1},{1,2},{2,3},{3,4},{4,5},{5,6},{6,7},{7,8},{8,9},{9,10},{10,1... | collective-permute-start | bytes 233480 | tf_op jit(solution)/shard_map/ppermute | solution.py:19
  55.1 0.7 copy-start.6
  55.1 0.9 copy-start.1
  55.1 29.7 %copy-start.4 = (f32[2,3,128]{2,0,1:T(2,128)S(1)}, f32[2,3,128]{2,0,1:T(2,128)}, u32[]{:S(2)}) copy-start(f32[2,3,128]{2,0,1:T(2,128)} %param.25) | copy-start | bytes 9220
  55.1 30.8 %copy-start.3 = (f32[3,1024]{1,0:T(4,128)S(1)}, f32[3,1024]{1,0:T(4,128)}, u32[]{:S(2)}) copy-start(f32[3,1024]{1,0:T(4,128)} %param.19) | copy-start | bytes 36868
  55.1 130.2 %reduce-scatter.6.cloned.1.call-start = ((), (), s32[]{:S(2)}) async-start(), calls=%async_computation.4 | async-start | bytes 278528 | tf_op jit(solution)/shard_map/reduce_scatter | solution.py:77
  116.0 39.9 %collective-permute-start.3 = (f32[19,1024]{1,0:T(8,128)S(1)}, f32[19,1024]{1,0:T(8,128)S(1)}, u32[]{:S(2)}, u32[]{:S(2)}) collective-permute-start(f32[19,1024]{1,0:T(8,128)S(1)} %pad_maximum_fusion.4), channel_id=1, source_target_pairs={{1,0},{2,1},{3,2},{4,3},{5,4},{6,5},{7,6},{8,7},{9,8},{10,9},{11,1... | collective-permute-start | bytes 233480 | tf_op jit(solution)/shard_map/ppermute | solution.py:20
  117.9 38.0 %collective-permute-start.2 = (f32[19,1024]{1,0:T(8,128)S(1)}, f32[19,1024]{1,0:T(8,128)S(1)}, u32[]{:S(2)}, u32[]{:S(2)}) collective-permute-start(f32[19,1024]{1,0:T(8,128)S(1)} %pad_maximum_fusion.4), channel_id=1, source_target_pairs={{0,1},{1,2},{2,3},{3,4},{4,5},{5,6},{6,7},{7,8},{8,9},{9,10},{10,1... | collective-permute-start | bytes 233480 | tf_op jit(solution)/shard_map/ppermute | solution.py:19
  124.4 132.9 %reduce-scatter.8.cloned.1.call-start = ((), (), s32[]{:S(2)}) async-start(), calls=%async_computation.5 | async-start | bytes 278528 | tf_op jit(solution)/shard_map/reduce_scatter | solution.py:77
  186.6 41.2 %collective-permute-start.5 = (f32[19,1024]{1,0:T(8,128)S(1)}, f32[19,1024]{1,0:T(8,128)S(1)}, u32[]{:S(2)}, u32[]{:S(2)}) collective-permute-start(f32[19,1024]{1,0:T(8,128)S(1)} %pad_maximum_fusion.5), channel_id=1, source_target_pairs={{1,0},{2,1},{3,2},{4,3},{5,4},{6,5},{7,6},{8,7},{9,8},{10,9},{11,1... | collective-permute-start | bytes 233480 | tf_op jit(solution)/shard_map/ppermute | solution.py:20
  188.5 39.3 %collective-permute-start.4 = (f32[19,1024]{1,0:T(8,128)S(1)}, f32[19,1024]{1,0:T(8,128)S(1)}, u32[]{:S(2)}, u32[]{:S(2)}) collective-permute-start(f32[19,1024]{1,0:T(8,128)S(1)} %pad_maximum_fusion.5), channel_id=1, source_target_pairs={{0,1},{1,2},{2,3},{3,4},{4,5},{5,6},{6,7},{7,8},{8,9},{9,10},{10,1... | collective-permute-start | bytes 233480 | tf_op jit(solution)/shard_map/ppermute | solution.py:19
Sparse Core Ops, SparseCore 0:
  55.2 56.6 reduce-scatter.3
  124.5 60.7 reduce-scatter.5
  195.1 62.1 reduce-scatter.7
where the time goes:
time: 313 us; the launch traced here: 312 us
  blocking collectives  175 us (56%)
  matrix products  66.6 us (21%)
  local copies, waits for them, and re-layouts  24.2 us (8%)
  loops' own time  13.7 us (4%)
  between operations  13.7 us (4%)
  starting transfers between devices  13.2 us (4%)
  other arithmetic  4.5 us (1%)
    psum x3, blocking collectives, operate(): subtree_total = lax.psum(upward, 'leaf')  79.1 us
    dot_general x18, matrix products, near_slot(): product = jnp.einsum('vlp,lpq->lvq', source_vecs, kernel, precision=highest)  50 us
    psum x1, blocking collectives, on_device(): lax.psum(jnp.sum(term_three * term_three, axis=1), ('grp', 'leaf'))  46.5 us
    all_gather x1, blocking collectives, on_device(): subtree_skel = lax.all_gather(skel_points, 'leaf', axis=0, tiled=True)  21.1 us
    all_gather x1, blocking collectives, on_device(): subtree_lists = lax.all_gather(inter_lists, 'leaf', axis=0, tiled=True)  15.5 us
    another operation x3, loops' own time, operate(): lax.fori_loop(0, live_slots, near_slot, jnp.zeros((per_dev, vec_count, le...  13.7 us
    all_gather x3, blocking collectives, operate(): lax.all_gather(subtree_total[None], 'grp', axis=0, tiled=True)  13.1 us
    dot_general x3, matrix products, operate(): jnp.einsum('jvr,tjrq->tvq', coeffs, push_kernel, precision=highest)  10.4 us
  transfers between devices with their start and end apart: 9, of which 2 were waited for; matrix products, arithmetic and copies ran while one was open for 29% of the time, Pallas kernels for 0%

commit v1 on v0

--- a/solution.py
+++ b/solution.py
@@ -81,7 +81,11 @@
             tiled=True,
         )
         upward = jnp.einsum("lvr,lrc->vc", coeffs, transfer, precision=highest)
-        subtree_total = lax.psum(upward, "leaf")
+        subtree_total = upward
+        for hop in (1, 2, 4, 8):
+            subtree_total = subtree_total + lax.ppermute(
+                subtree_total, "leaf", [(dev, dev ^ hop) for dev in range(16)]
+            )
         group_coeffs = lax.all_gather(subtree_total[None], "grp", axis=0, tiled=True)
         coarse_field = jnp.einsum("avr,arq->vq", group_coeffs, coupling, precision=highest)
         downward = leaf_far + jnp.einsum("vc,lrc->lvr", coarse_field, transfer, precision=highest)

time: 313 us -> 309 us (0.987)
  blocking collectives: 175 us -> 89.7 us
  waiting for transfers between devices: 1.34 us -> 69.5 us
  starting transfers between devices: 13.2 us -> 23.6 us
    psum x3 -> x0, blocking collectives: 79.1 us -> none  [operate(): subtree_total = lax.psum(upward, 'leaf')]
    reduce_scatter x3, waiting for transfers between devices: 1.24 us -> 52.9 us  [operate(): lax.psum_scatter(jnp.einsum('jvr,tjrq->tvq', coeffs, push_kernel, precisi...]
    ppermute x0 -> x12, waiting for transfers between devices: none -> 16.6 us  [operate(): lax.ppermute(subtree_total, 'leaf', [(dev, dev ^ hop) for dev in range(16)])]
    ppermute x0 -> x12, starting transfers between devices: none -> 10.4 us  [operate(): lax.ppermute(subtree_total, 'leaf', [(dev, dev ^ hop) for dev in range(16)])]
    psum x1, blocking collectives: 46.5 us -> 40 us  [on_device(): lax.psum(jnp.sum(term_three * term_three, axis=1), ('grp', 'leaf'))]
  transfers between devices with their start and end apart: 9 -> 21, of which waited for: 2 -> 11; matrix products, arithmetic and copies ran while one was open for 29% -> 29% of each run, Pallas kernels for 0% -> 0%
where the time goes in v1:
time: 309 us; the launch traced here: 306 us
  blocking collectives  89.7 us (29%)
  waiting for transfers between devices  69.5 us (22%)
  matrix products  66.6 us (22%)
  local copies, waits for them, and re-layouts  23.7 us (8%)
  starting transfers between devices  23.6 us (8%)
  loops' own time  14.9 us (5%)
  between operations  13.8 us (4%)
  other arithmetic  4.6 us (1%)
    reduce_scatter x3, waiting for transfers between devices, operate(): lax.psum_scatter(jnp.einsum('jvr,tjrq->tvq', coeffs, push_kernel, precisi...  52.9 us
    dot_general x18, matrix products, near_slot(): product = jnp.einsum('vlp,lpq->lvq', source_vecs, kernel, precision=highest)  50 us
    psum x1, blocking collectives, on_device(): lax.psum(jnp.sum(term_three * term_three, axis=1), ('grp', 'leaf'))  40 us
    all_gather x1, blocking collectives, on_device(): subtree_skel = lax.all_gather(skel_points, 'leaf', axis=0, tiled=True)  21.1 us
    ppermute x12, waiting for transfers between devices, operate(): lax.ppermute(subtree_total, 'leaf', [(dev, dev ^ hop) for dev in range(16)])  16.6 us
    all_gather x1, blocking collectives, on_device(): subtree_lists = lax.all_gather(inter_lists, 'leaf', axis=0, tiled=True)  15.5 us
    another operation x3, loops' own time, operate(): lax.fori_loop(0, live_slots, near_slot, jnp.zeros((per_dev, vec_count, le...  14.9 us
    all_gather x3, blocking collectives, operate(): lax.all_gather(subtree_total[None], 'grp', axis=0, tiled=True)  13.1 us
  transfers between devices with their start and end apart: 21, of which 11 were waited for; matrix products, arithmetic and copies ran while one was open for 29% of the time, Pallas kernels for 0%

profile of v1, /device:TPU:10, one launch (start us, length us, event | category | flops | bytes accessed | tf_op | source)
XLA Modules:
  0.0 306.4 jit_solution(5130244202178165832)
XLA Ops:
  6.5 0.9 pad_maximum_fusion.3
  7.5 2.1 collective-permute-start.1
  9.5 2.4 collective-permute-start
  11.9 0.9 copy.61
  13.0 1.2 gather_fusion.6
  14.4 15.5 %all-gather.3 = s32[16,2,16]{2,1,0:T(2,128)S(1)} all-gather(s32[1,2,16]{2,1,0:T(2,128)S(1)} %bitcast.263), channel_id=1, replica_groups=mesh['grp'=2,'leaf'=16] {'leaf'}, dimensions={0}, use_global_device_ids=true | all-gather | bytes 2176 | tf_op jit(solution)/shard_map/all_gather | solution.py:49
  30.1 21.1 %all_gather.15 = f32[32,3,64]{2,1,0:T(4,128)S(1)} all-gather(f32[2,3,64]{2,1,0:T(4,128)S(1)} %bitcast_select_fusion.1), channel_id=1, replica_groups=mesh['grp'=2,'leaf'=16] {'leaf'}, dimensions={0}, use_global_device_ids=true | all-gather | bytes 26112 | tf_op jit(solution)/shard_map/all_gather | solution.py:43
  51.6 3.5 %convolution_bitcast_fusion.2 = f32[32,16,64]{2,1,0:T(8,128)} fusion(f32[32,2]{1,0:T(8,128)S(1)} %copy.67, f32[32,64]{1,0:T(8,128)S(1)} %bitcast.257, f32[2,64]{1,0:T(2,128)S(1)} %bitcast.267, f32[32,64]{1,0:T(8,128)S(1)} %bitcast.260, f32[2,64]{1,0:T(2,128)S(1)} %bitcast.270, f32[32,64]{1,0:T(8,128)S(1)} %bitcast.254, f32[2,64]{1,0:T(2,128)S(1)} %bitcast.264, ...), kind=kOutput, calls=%fused_computation.145 | convolution fusion | flops 53739520 | bytes 165632 | tf_op jit(solution)/shard_map/jvr,tjrq->tvq/dot_general | solution.py:78
  55.7 0.8 collective-permute-done.2
  57.0 3.2 %collective-permute-done.3 = f32[16,128]{1,0:T(8,128)S(1)} collective-permute-done((f32[16,128]{1,0:T(8,128)S(1)}, f32[16,128]{1,0:T(8,128)S(1)}, u32[]{:S(2)}, u32[]{:S(2)}) %collective-permute-start.3) | collective-permute-done | bytes 8224 | tf_op jit(solution)/shard_map/ppermute | solution.py:86
  60.2 3.3 %collective-permute-start.4 = (f32[16,128]{1,0:T(8,128)S(1)}, f32[16,128]{1,0:T(8,128)S(1)}, u32[]{:S(2)}, u32[]{:S(2)}) collective-permute-start(f32[16,128]{1,0:T(8,128)S(1)} %add.182), channel_id=1, source_target_pairs={{0,4},{1,5},{2,6},{3,7},{4,0},{5,1},{6,2},{7,3},{8,12},{9,13},{10,... | collective-permute-start | bytes 24584 | tf_op jit(solution)/shard_map/ppermute | solution.py:86
  63.5 1.6 collective-permute-done.4
  65.1 1.1 collective-permute-start.5
  66.5 0.7 reduce_max.9
  67.2 2.4 collective-permute-done.5
  69.7 4.3 %all-gather = f32[32,128]{1,0:T(8,128)S(1)} all-gather(f32[16,128]{1,0:T(8,128)S(1)} %add.184), channel_id=2, replica_groups=mesh['grp'=2,'leaf'=16] {'grp'}, dimensions={0}, use_global_device_ids=true | all-gather | bytes 24576 | tf_op jit(solution)/shard_map/all_gather | solution.py:89
  74.5 29.0 %while.30 = (s32[]{:T(128)}, f32[2,16,512]{2,1,0:T(8,128)S(1)}, s32[]{:T(128)}, s32[2,6]{0,1:T(8,128)S(1)}, f32[16,6,512]{2,0,1:T(8,128)S(1)}, /*index=5*/f32[3,...) while((s32[]{:T(128)}, f32[2,16,512]{2,1,0:T(8,128)S(1)}, s32[]{:T(128)}, ...), condition=%wide.region_3.0_spmd, body=%wide.region_2.0_spmd.sunk | while | flops 107008024 | bytes 479441 | solution.py:72
  75.2 0.6 gather_fusion
  76.5 2.8 fusion.199
  79.9 0.6 gather_fusion
  81.2 2.8 fusion.199
  84.7 0.6 gather_fusion
  85.9 2.8 fusion.199
  89.4 0.6 gather_fusion
  90.7 2.8 fusion.199
  95.4 2.8 fusion.199
  100.1 2.8 fusion.199
  103.6 8.4 %reduce-scatter.4.cloned.1.call-done = f32[2,16,64]{2,1,0:T(8,128)} async-done(((f32[32,16,64]{2,1,0:T(8,128)}), f32[2,16,64]{2,1,0:T(8,128)}) %reduce-scatter.4.cloned.1.call-update) | async-done | bytes 8208 | tf_op jit(solution)/shard_map/reduce_scatter | solution.py:77
  111.9 0.9 fusion.116
  113.8 1.2 collective-permute-done.8
  115.5 3.1 %collective-permute-done.9 = f32[16,128]{1,0:T(8,128)S(1)} collective-permute-done((f32[16,128]{1,0:T(8,128)S(1)}, f32[16,128]{1,0:T(8,128)S(1)}, u32[]{:S(2)}, u32[]{:S(2)}) %collective-permute-start.9) | collective-permute-done | bytes 8224 | tf_op jit(solution)/shard_map/ppermute | solution.py:86
  119.1 1.9 collective-permute-start.7
  121.1 2.4 collective-permute-start.6
  123.5 1.6 collective-permute-start.11
  125.1 3.4 %convolution_bitcast_fusion.1 = f32[32,16,64]{2,1,0:T(8,128)} fusion(f32[32,2]{1,0:T(8,128)S(1)} %copy.67, f32[32,64]{1,0:T(8,128)S(1)} %bitcast.258, f32[2,64]{1,0:T(2,128)S(1)} %bitcast.268, f32[32,64]{1,0:T(8,128)S(1)} %bitcast.261, f32[2,64]{1,0:T(2,128)S(1)} %bitcast.271, f32[32,64]{1,0:T(8,128)S(1)} %bitcast.255, f32[2,64]{1,0:T(2,128)S(1)} %bitcast.265, ...), kind=kOutput, calls=%fused_computation.144 | convolution fusion | flops 53739520 | bytes 165632 | tf_op jit(solution)/shard_map/jvr,tjrq->tvq/dot_general | solution.py:78
  128.6 4.4 %all-gather.1 = f32[32,128]{1,0:T(8,128)S(1)} all-gather(f32[16,128]{1,0:T(8,128)S(1)} %add.195), channel_id=3, replica_groups=mesh['grp'=2,'leaf'=16] {'grp'}, dimensions={0}, use_global_device_ids=true | all-gather | bytes 24576 | tf_op jit(solution)/shard_map/all_gather | solution.py:89
  133.5 29.2 %while.31 = (s32[]{:T(128)}, f32[2,16,512]{2,1,0:T(8,128)S(1)}, s32[]{:T(128)}, s32[2,6]{0,1:T(8,128)S(1)}, f32[16,6,512]{2,0,1:T(8,128)S(1)}, /*index=5*/f32[3,...) while((s32[]{:T(128)}, f32[2,16,512]{2,1,0:T(8,128)S(1)}, s32[]{:T(128)}, ...), condition=%wide.region_7.10_spmd, body=%wide.region_6.9_spmd.sunk | while | flops 107008024 | bytes 479441 | solution.py:72
  135.6 2.8 fusion.203
  140.3 2.8 fusion.203
  145.1 2.8 fusion.203
  149.8 2.8 fusion.203
  154.5 2.8 fusion.203
  159.3 2.8 fusion.203
  162.7 22.2 %reduce-scatter.6.cloned.1.call-done = f32[2,16,64]{2,1,0:T(8,128)} async-done(((f32[32,16,64]{2,1,0:T(8,128)}), f32[2,16,64]{2,1,0:T(8,128)}) %reduce-scatter.6.cloned.1.call-update) | async-done | bytes 8208 | tf_op jit(solution)/shard_map/reduce_scatter | solution.py:77
  184.9 0.9 fusion.115
  186.7 1.2 collective-permute-done.14
  188.4 3.1 %collective-permute-done.15 = f32[16,128]{1,0:T(8,128)S(1)} collective-permute-done((f32[16,128]{1,0:T(8,128)S(1)}, f32[16,128]{1,0:T(8,128)S(1)}, u32[]{:S(2)}, u32[]{:S(2)}) %collective-permute-start.15) | collective-permute-done | bytes 8224 | tf_op jit(solution)/shard_map/ppermute | solution.py:86
  191.5 0.6 collective-permute-start.16
  192.1 1.9 collective-permute-start.13
  194.0 2.4 collective-permute-start.12
  196.5 1.6 collective-permute-start.17
  198.0 3.4 %convolution_bitcast_fusion = f32[32,16,64]{2,1,0:T(8,128)} fusion(f32[32,2]{1,0:T(8,128)S(1)} %copy.67, f32[32,64]{1,0:T(8,128)S(1)} %bitcast.259, f32[2,64]{1,0:T(2,128)S(1)} %bitcast.269, f32[32,64]{1,0:T(8,128)S(1)} %bitcast.262, f32[2,64]{1,0:T(2,128)S(1)} %bitcast.272, f32[32,64]{1,0:T(8,128)S(1)} %bitcast.256, f32[2,64]{1,0:T(2,128)S(1)} %bitcast.266, ...), kind=kOutput, calls=%fused_computation.143 | convolution fusion | flops 53739520 | bytes 165632 | tf_op jit(solution)/shard_map/jvr,tjrq->tvq/dot_general | solution.py:78
  201.5 4.4 %all-gather.2 = f32[32,128]{1,0:T(8,128)S(1)} all-gather(f32[16,128]{1,0:T(8,128)S(1)} %add.201), channel_id=4, replica_groups=mesh['grp'=2,'leaf'=16] {'grp'}, dimensions={0}, use_global_device_ids=true | all-gather | bytes 24576 | tf_op jit(solution)/shard_map/all_gather | solution.py:89
  206.4 29.0 %while.32 = (s32[]{:T(128)}, f32[2,16,512]{2,1,0:T(8,128)S(1)}, s32[]{:T(128)}, s32[2,6]{0,1:T(8,128)S(1)}, f32[16,6,512]{2,0,1:T(8,128)S(1)}, /*index=5*/f32[3,...) while((s32[]{:T(128)}, f32[2,16,512]{2,1,0:T(8,128)S(1)}, s32[]{:T(128)}, ...), condition=%wide.region_10.13_spmd, body=%wide.region_9.12_spmd.sunk | while | flops 107008024 | bytes 479441 | solution.py:72
  208.3 2.8 fusion.207
  213.0 2.8 fusion.207
  217.8 2.8 fusion.207
  222.5 2.8 fusion.207
  227.3 2.8 fusion.207
  232.0 2.8 fusion.207
  235.4 22.3 %reduce-scatter.8.cloned.1.call-done = f32[2,16,64]{2,1,0:T(8,128)} async-done(((f32[32,16,64]{2,1,0:T(8,128)}), f32[2,16,64]{2,1,0:T(8,128)}) %reduce-scatter.8.cloned.1.call-update) | async-done | bytes 8208 | tf_op jit(solution)/shard_map/reduce_scatter | solution.py:77
  257.8 0.9 fusion.114
  259.1 40.0 %psum.7 = f32[16]{0:T(128)S(1)} all-reduce(f32[16]{0:T(128)S(1)} %multiply_reduce_fusion), channel_id=1, replica_groups=mesh['grp'=2,'leaf'=16] {'grp','leaf'}, use_global_device_ids=true, to_apply=%region_13.16 | all-reduce | flops 16 | bytes 128 | tf_op jit(solution)/shard_map/psum | solution.py:99
  299.1 0.7 broadcast_divide_fusion
  (245 shorter events, 27.4 us)
Async XLA Ops:
  6.5 44.8 %copy-start = (f32[2,64,512]{2,1,0:T(8,128)S(1)}, f32[2,64,512]{2,1,0:T(8,128)}, u32[]{:S(2)}) copy-start(f32[2,64,512]{2,1,0:T(8,128)} %param.23) | copy-start | bytes 786436
  6.5 6.4 %copy-start.7 = (s32[2,64]{1,0:T(2,128)S(1)}, s32[2,64]{1,0:T(2,128)}, u32[]{:S(2)}) copy-start(s32[2,64]{1,0:T(2,128)} %param.22) | copy-start | bytes 1540
  6.5 7.8 %copy-start.5 = (s32[2,16]{1,0:T(2,128)S(1)}, s32[2,16]{1,0:T(2,128)}, u32[]{:S(2)}) copy-start(s32[2,16]{1,0:T(2,128)} %param.21) | copy-start | bytes 388
  6.5 105.4 %reduce-scatter.4.cloned.1.call-start = ((), (), s32[]{:S(2)}) async-start(), calls=%async_computation.3 | async-start | bytes 278528 | tf_op jit(solution)/shard_map/reduce_scatter | solution.py:77
  7.5 43.8 %copy-start.2 = (f32[16,1024]{1,0:T(8,128)S(1)}, f32[16,1024]{1,0:T(8,128)}, u32[]{:S(2)}) copy-start(f32[16,1024]{1,0:T(8,128)} %param.18) | copy-start | bytes 196612
  7.5 66.9 %collective-permute-start.1 = (f32[19,1024]{1,0:T(8,128)S(1)}, f32[19,1024]{1,0:T(8,128)S(1)}, u32[]{:S(2)}, u32[]{:S(2)}) collective-permute-start(f32[19,1024]{1,0:T(8,128)S(1)} %pad_maximum_fusion.3), channel_id=1, source_target_pairs={{1,0},{2,1},{3,2},{4,3},{5,4},{6,5},{7,6},{8,7},{9,8},{10,9},{11,1... | collective-permute-start | bytes 233480 | tf_op jit(solution)/shard_map/ppermute | solution.py:20
  9.5 64.9 %collective-permute-start = (f32[19,1024]{1,0:T(8,128)S(1)}, f32[19,1024]{1,0:T(8,128)S(1)}, u32[]{:S(2)}, u32[]{:S(2)}) collective-permute-start(f32[19,1024]{1,0:T(8,128)S(1)} %pad_maximum_fusion.3), channel_id=1, source_target_pairs={{0,1},{1,2},{2,3},{3,4},{4,5},{5,6},{6,7},{7,8},{8,9},{9,10},{10,1... | collective-permute-start | bytes 233480 | tf_op jit(solution)/shard_map/ppermute | solution.py:19
  51.6 3.6 %copy-start.1 = (f32[2,64,128]{2,1,0:T(8,128)S(1)}, f32[2,64,128]{2,1,0:T(8,128)}, u32[]{:S(2)}) copy-start(f32[2,64,128]{2,1,0:T(8,128)} %param.24) | copy-start | bytes 196612
  51.6 4.1 %copy-start.4 = (f32[2,3,128]{2,0,1:T(2,128)S(1)}, f32[2,3,128]{2,0,1:T(2,128)}, u32[]{:S(2)}) copy-start(f32[2,3,128]{2,0,1:T(2,128)} %param.25) | copy-start | bytes 9220
  51.6 5.3 %copy-start.6 = (s32[2,6]{1,0:T(2,128)S(1)}, s32[2,6]{1,0:T(2,128)}, u32[]{:S(2)}) copy-start(s32[2,6]{1,0:T(2,128)} %param.20) | copy-start | bytes 148
  55.1 129.7 %reduce-scatter.6.cloned.1.call-start = ((), (), s32[]{:S(2)}) async-start(), calls=%async_computation.4 | async-start | bytes 278528 | tf_op jit(solution)/shard_map/reduce_scatter | solution.py:77
  55.4 1.2 collective-permute-start.2
  56.6 3.7 %collective-permute-start.3 = (f32[16,128]{1,0:T(8,128)S(1)}, f32[16,128]{1,0:T(8,128)S(1)}, u32[]{:S(2)}, u32[]{:S(2)}) collective-permute-start(f32[16,128]{1,0:T(8,128)S(1)} %add.181), channel_id=1, source_target_pairs={{0,2},{1,3},{2,0},{3,1},{4,6},{5,7},{6,4},{7,5},{8,10},{9,11},{10,... | collective-permute-start | bytes 24584 | tf_op jit(solution)/shard_map/ppermute | solution.py:86
  60.2 4.9 %collective-permute-start.4 = (f32[16,128]{1,0:T(8,128)S(1)}, f32[16,128]{1,0:T(8,128)S(1)}, u32[]{:S(2)}, u32[]{:S(2)}) collective-permute-start(f32[16,128]{1,0:T(8,128)S(1)} %add.182), channel_id=1, source_target_pairs={{0,4},{1,5},{2,6},{3,7},{4,0},{5,1},{6,2},{7,3},{8,12},{9,13},{10,... | collective-permute-start | bytes 24584 | tf_op jit(solution)/shard_map/ppermute | solution.py:86
  65.1 4.5 %collective-permute-start.5 = (f32[16,128]{1,0:T(8,128)S(1)}, f32[16,128]{1,0:T(8,128)S(1)}, u32[]{:S(2)}, u32[]{:S(2)}) collective-permute-start(f32[16,128]{1,0:T(8,128)S(1)} %add.183), channel_id=1, source_target_pairs={{0,8},{1,9},{2,10},{3,11},{4,12},{5,13},{6,14},{7,15},{8,0},{9,1},... | collective-permute-start | bytes 24584 | tf_op jit(solution)/shard_map/ppermute | solution.py:86
  66.3 8.1 %copy-start.3 = (f32[3,1024]{1,0:T(4,128)S(1)}, f32[3,1024]{1,0:T(4,128)}, u32[]{:S(2)}) copy-start(f32[3,1024]{1,0:T(4,128)} %param.19) | copy-start | bytes 36868
  113.8 1.2 collective-permute-start.8
  114.9 3.7 %collective-permute-start.9 = (f32[16,128]{1,0:T(8,128)S(1)}, f32[16,128]{1,0:T(8,128)S(1)}, u32[]{:S(2)}, u32[]{:S(2)}) collective-permute-start(f32[16,128]{1,0:T(8,128)S(1)} %add.192), channel_id=1, source_target_pairs={{0,2},{1,3},{2,0},{3,1},{4,6},{5,7},{6,4},{7,5},{8,10},{9,11},{10,... | collective-permute-start | bytes 24584 | tf_op jit(solution)/shard_map/ppermute | solution.py:86
  118.6 4.9 %collective-permute-start.10 = (f32[16,128]{1,0:T(8,128)S(1)}, f32[16,128]{1,0:T(8,128)S(1)}, u32[]{:S(2)}, u32[]{:S(2)}) collective-permute-start(f32[16,128]{1,0:T(8,128)S(1)} %add.193), channel_id=1, source_target_pairs={{0,4},{1,5},{2,6},{3,7},{4,0},{5,1},{6,2},{7,3},{8,12},{9,13},{10,... | collective-permute-start | bytes 24584 | tf_op jit(solution)/shard_map/ppermute | solution.py:86
  119.1 14.2 %collective-permute-start.7 = (f32[19,1024]{1,0:T(8,128)S(1)}, f32[19,1024]{1,0:T(8,128)S(1)}, u32[]{:S(2)}, u32[]{:S(2)}) collective-permute-start(f32[19,1024]{1,0:T(8,128)S(1)} %pad_maximum_fusion.4), channel_id=1, source_target_pairs={{1,0},{2,1},{3,2},{4,3},{5,4},{6,5},{7,6},{8,7},{9,8},{10,9},{11,1... | collective-permute-start | bytes 233480 | tf_op jit(solution)/shard_map/ppermute | solution.py:20
  121.1 12.3 %collective-permute-start.6 = (f32[19,1024]{1,0:T(8,128)S(1)}, f32[19,1024]{1,0:T(8,128)S(1)}, u32[]{:S(2)}, u32[]{:S(2)}) collective-permute-start(f32[19,1024]{1,0:T(8,128)S(1)} %pad_maximum_fusion.4), channel_id=1, source_target_pairs={{0,1},{1,2},{2,3},{3,4},{4,5},{5,6},{6,7},{7,8},{8,9},{9,10},{10,1... | collective-permute-start | bytes 233480 | tf_op jit(solution)/shard_map/ppermute | solution.py:19
  123.5 5.1 %collective-permute-start.11 = (f32[16,128]{1,0:T(8,128)S(1)}, f32[16,128]{1,0:T(8,128)S(1)}, u32[]{:S(2)}, u32[]{:S(2)}) collective-permute-start(f32[16,128]{1,0:T(8,128)S(1)} %add.194), channel_id=1, source_target_pairs={{0,8},{1,9},{2,10},{3,11},{4,12},{5,13},{6,14},{7,15},{8,0},{9,1},... | collective-permute-start | bytes 24584 | tf_op jit(solution)/shard_map/ppermute | solution.py:86
  128.5 129.2 %reduce-scatter.8.cloned.1.call-start = ((), (), s32[]{:S(2)}) async-start(), calls=%async_computation.5 | async-start | bytes 278528 | tf_op jit(solution)/shard_map/reduce_scatter | solution.py:77
  186.7 1.2 collective-permute-start.14
  187.8 3.7 %collective-permute-start.15 = (f32[16,128]{1,0:T(8,128)S(1)}, f32[16,128]{1,0:T(8,128)S(1)}, u32[]{:S(2)}, u32[]{:S(2)}) collective-permute-start(f32[16,128]{1,0:T(8,128)S(1)} %add.198), channel_id=1, source_target_pairs={{0,2},{1,3},{2,0},{3,1},{4,6},{5,7},{6,4},{7,5},{8,10},{9,11},{10,... | collective-permute-start | bytes 24584 | tf_op jit(solution)/shard_map/ppermute | solution.py:86
  191.5 4.9 %collective-permute-start.16 = (f32[16,128]{1,0:T(8,128)S(1)}, f32[16,128]{1,0:T(8,128)S(1)}, u32[]{:S(2)}, u32[]{:S(2)}) collective-permute-start(f32[16,128]{1,0:T(8,128)S(1)} %add.199), channel_id=1, source_target_pairs={{0,4},{1,5},{2,6},{3,7},{4,0},{5,1},{6,2},{7,3},{8,12},{9,13},{10,... | collective-permute-start | bytes 24584 | tf_op jit(solution)/shard_map/ppermute | solution.py:86
  192.1 14.2 %collective-permute-start.13 = (f32[19,1024]{1,0:T(8,128)S(1)}, f32[19,1024]{1,0:T(8,128)S(1)}, u32[]{:S(2)}, u32[]{:S(2)}) collective-permute-start(f32[19,1024]{1,0:T(8,128)S(1)} %pad_maximum_fusion.5), channel_id=1, source_target_pairs={{1,0},{2,1},{3,2},{4,3},{5,4},{6,5},{7,6},{8,7},{9,8},{10,9},{11,1... | collective-permute-start | bytes 233480 | tf_op jit(solution)/shard_map/ppermute | solution.py:20
  194.0 12.2 %collective-permute-start.12 = (f32[19,1024]{1,0:T(8,128)S(1)}, f32[19,1024]{1,0:T(8,128)S(1)}, u32[]{:S(2)}, u32[]{:S(2)}) collective-permute-start(f32[19,1024]{1,0:T(8,128)S(1)} %pad_maximum_fusion.5), channel_id=1, source_target_pairs={{0,1},{1,2},{2,3},{3,4},{4,5},{5,6},{6,7},{7,8},{8,9},{9,10},{10,1... | collective-permute-start | bytes 233480 | tf_op jit(solution)/shard_map/ppermute | solution.py:19
  196.5 5.0 %collective-permute-start.17 = (f32[16,128]{1,0:T(8,128)S(1)}, f32[16,128]{1,0:T(8,128)S(1)}, u32[]{:S(2)}, u32[]{:S(2)}) collective-permute-start(f32[16,128]{1,0:T(8,128)S(1)} %add.200), channel_id=1, source_target_pairs={{0,8},{1,9},{2,10},{3,11},{4,12},{5,13},{6,14},{7,15},{8,0},{9,1},... | collective-permute-start | bytes 24584 | tf_op jit(solution)/shard_map/ppermute | solution.py:86
Sparse Core Ops, SparseCore 0:
  55.2 56.6 reduce-scatter.3
  128.7 56.1 reduce-scatter.5
  201.6 56.0 reduce-scatter.7
